TPU v7x, 512 devices: a whole 4x4x16 slice. The times are simulated.
512 devices in a mesh: row: 32 (over y, x, core), col: 16 (over z).
Axes of the slice: x: 4, y: 4, z: 16, core: 2. Of those that a mesh axis runs over, the one named last changes fastest.
Arguments:
- a_tile: bfloat16 [8192, 16384], P('row', 'col'), may hold values from -6 to 6
- b_tile: bfloat16 [16384, 26624], P('row', 'col'), may hold values from -0.046875 to 0.046875
- c_prior: bfloat16 [8192, 26624], P('row', 'col'), may hold values from -0.29882812 to 0.29882812
- sketch_matrix: bfloat16 [26624, 128], P('col'), may hold values from -0.0390625 to 0.0390625
- panel_ids: int32 [2], replicated, may hold values from 0 to 31
Outputs:
- c_out: bfloat16 [8192, 26624], P('row', 'col')
- sketch: float32 [8192, 128], P('row')
- predicted: float32 [8192, 128], P('row')
Inputs may be any that keep to these rules, and one draw needn't show every extreme that they name: `panel_ids`: the 2 ids may repeat.
All inputs are finite; a program needn't handle non-finite values.
Results may differ from a plain program's by a relative error of at most 0.0029.
Values may be sent and summed in bfloat16 or wider, within the bound.
A program may use at most 64 MiB of HBM per device.

v0:
```python
import jax
import jax.numpy as jnp
from jax import lax
from jax.sharding import PartitionSpec as P

PANEL = 512
STEPS = 2


def broadcast(value, axis, source):
    kept = jnp.where(lax.axis_index(axis) == source, value, 0).astype(value.dtype)
    return lax.psum(kept, axis)


def locate_pieces(a_tile, b_tile, panel_ids, step):
    first_row = panel_ids[step] * PANEL
    a_width = a_tile.shape[1]
    b_height = b_tile.shape[0]
    a_owner = first_row // a_width
    b_owner = first_row // b_height
    a_piece = lax.dynamic_slice_in_dim(a_tile, first_row - a_owner * a_width, PANEL, 1)
    return (a_piece, a_owner, b_tile, b_owner)


def spread_activations(a_piece, a_owner):
    return broadcast(a_piece, "col", a_owner)


def spread_weights(b_piece, b_owner):
    return broadcast(b_piece, "row", b_owner)


def panel_terms(a_panel, b_panel, sketch_matrix):
    product = jnp.dot(a_panel, b_panel, preferred_element_type=jnp.float32)
    local_sketch = jnp.dot(b_panel, sketch_matrix, preferred_element_type=jnp.float32)
    local_sketch = lax.psum(local_sketch, "col")
    predicted_term = jnp.dot(
        a_panel.astype(jnp.float32), local_sketch, precision=lax.Precision.HIGHEST
    )
    return (product, predicted_term)


def per_device(a_tile, b_tile, c_prior, sketch_matrix, panel_ids):
    located = [locate_pieces(a_tile, b_tile, panel_ids, step) for step in range(STEPS)]
    a_panels = [spread_activations(entry[0], entry[1]) for entry in located]
    b_panels = [spread_weights(entry[2], entry[3]) for entry in located]
    running = c_prior.astype(jnp.float32)
    predicted_part = jnp.zeros((c_prior.shape[0], sketch_matrix.shape[1]), jnp.float32)
    for step in range(STEPS):
        product, predicted_term = panel_terms(a_panels[step], b_panels[step], sketch_matrix)
        running = running + product
        predicted_part = predicted_part + predicted_term
    c_out = running.astype(jnp.bfloat16)
    local_sketch = jnp.dot(c_out, sketch_matrix, preferred_element_type=jnp.float32)
    sketch = lax.psum(local_sketch, "col")
    return (c_out, sketch, predicted_part)


def solution(mesh):
    placed = (P("row", "col"), P("row", "col"), P("row", "col"), P("col", None), P())
    return jax.shard_map(
        per_device,
        mesh=mesh,
        in_specs=placed,
        out_specs=(P("row", "col"), P("row", None), P("row", None)),
        check_vma=False,
    )
```

profile of v0, /device:TPU:2, one launch (start us, length us, event | category | flops | bytes accessed | tf_op | source)
XLA Modules:
  0.0 449.5 jit_solution(555051361735433160)
XLA Ops:
  7.2 0.0 copy-start
  7.2 0.0 all-reduce.9.cloned.1.call-start
  7.2 1.3 fusion.1
  9.9 3.5 broadcast_select_fusion
  13.4 0.0 all-reduce.9.cloned.1.call-update
  13.4 0.0 all-reduce.11.cloned.1.call-start
  13.5 0.9 copy-done.6
  14.4 0.9 dynamic-slice_select_fusion
  15.3 0.0 all-reduce.11.cloned.1.call-update
  15.3 0.0 all-reduce.7.cloned.1.call-start
  15.4 142.3 %all-reduce.9.cloned.1.call-done = (bf16[512,1664]{1,0:T(8,128)(2,1)}, bf16[512,1664]{1,0:T(8,128)(2,1)}) async-done(((bf16[512,1664]{1,0:T(8,128)(2,1)}, bf16[512,1664]{1,0:T(8,128)(2,1)}), (bf16[512,1664]{1,0:T(8,128)(2,1)}, bf16[512,1664]{1,0:T(8,128)(2,1)})) %all-reduce.9.cloned.1.call-update) | async-done | bytes 3407888 | tf_op jit(solution)/shard_map/psum | solution.py:12
  157.7 2.9 fusion.3
  160.6 1.3 fusion.5
  161.9 137.1 %all-reduce.11.cloned.1.call-done = (bf16[256,512]{1,0:T(8,128)(2,1)}, bf16[256,512]{1,0:T(8,128)(2,1)}) async-done(((bf16[256,512]{1,0:T(8,128)(2,1)}, bf16[256,512]{1,0:T(8,128)(2,1)}), (bf16[256,512]{1,0:T(8,128)(2,1)}, bf16[256,512]{1,0:T(8,128)(2,1)})) %all-reduce.11.cloned.1.call-update) | async-done | bytes 524304 | tf_op jit(solution)/shard_map/psum | solution.py:12
  299.0 0.0 copy-done.5
  299.0 2.2 convolution_add_fusion.1
  301.3 0.7 fusion
  301.9 0.0 copy-start.2
  302.0 1.0 fusion.2
  303.0 0.0 all-reduce.7.cloned.1.call-update
  303.0 135.1 %all-reduce.7.cloned.1.call-done = (f32[256,128]{1,0:T(8,128)}, f32[512,128]{1,0:T(8,128)}, f32[512,128]{1,0:T(8,128)}) async-done(((f32[256,128]{1,0:T(8,128)}, f32[512,128]{1,0:T(8,128)}, f32[512,128]{1,0:T(8,128)}), (f32[256,128]{1,0:T(8,128)}, f32[512,128]{1,0:T(8,128)}, f32[512,128]{1,0:T(8,128)})) %all-reduce.7.cloned.1.call-update) | async-done | bytes 655376 | tf_op jit(solution)/shard_map/psum | solution.py:55
  438.1 1.3 fusion.4
  439.4 2.0 convolution_add_fusion.2
  441.4 1.6 copy.15
  (10 shorter events, 0.0 us)
Async XLA Ops:
  7.2 150.5 %copy-start = (bf16[1664,128]{1,0:T(8,128)(2,1)S(1)}, bf16[1664,128]{1,0:T(8,128)(2,1)}, u32[]{:S(2)}) copy-start(bf16[1664,128]{1,0:T(8,128)(2,1)} %param.8) | copy-start | bytes 1277956
  7.2 150.5 %all-reduce.9.cloned.1.call-start = ((), (), s32[]{:S(2)}) async-start(), calls=%async_computation.1 | async-start | bytes 6815744 | tf_op jit(solution)/shard_map/psum | solution.py:12
  13.4 1.0 copy-start.6
  13.4 285.6 %all-reduce.11.cloned.1.call-start = ((), (), s32[]{:S(2)}) async-start(), calls=%async_computation.2 | async-start | bytes 1048576 | tf_op jit(solution)/shard_map/psum | solution.py:12
  15.3 422.8 %all-reduce.7.cloned.1.call-start = ((), (), s32[]{:S(2)}) async-start(), calls=%async_computation | async-start | bytes 1310720 | tf_op jit(solution)/shard_map/psum | solution.py:55
  157.7 2.9 copy-start.1
  160.6 138.4 %copy-start.5 = (bf16[256,1664]{1,0:T(8,128)(2,1)S(1)}, bf16[256,1664]{1,0:T(8,128)(2,1)}, u32[]{:S(2)}) copy-start(bf16[256,1664]{1,0:T(8,128)(2,1)} %param.7) | copy-start | bytes 2555908
  299.0 2.2 copy-start.3
  301.9 139.5 %copy-start.2 = (bf16[256,1664]{1,0:T(8,128)(2,1)}, bf16[256,1664]{1,0:T(8,128)(2,1)S(1)}, u32[]{:S(2)}) copy-start(bf16[256,1664]{1,0:T(8,128)(2,1)S(1)} %fusion) | copy-start | bytes 2555908
  301.9 136.1 %copy-start.4 = (bf16[256,512]{1,0:T(8,128)(2,1)S(1)}, bf16[256,512]{1,0:T(8,128)(2,1)}, u32[]{:S(2)}) copy-start(bf16[256,512]{1,0:T(8,128)(2,1)} %get-tuple-element.8) | copy-start | bytes 786436
Sparse Core Ops, SparseCore 0:
  13.5 144.1 all-reduce.8
  160.6 138.3 all-reduce.10
  303.1 134.9 all-reduce.6
where the time goes:
time: 450 us
  waiting for transfers between devices  415 us (92%)
  between operations  15.2 us (3%)
  matrix products  11.5 us (3%)
    psum x2, waiting for transfers between devices, broadcast(): return lax.psum(kept, axis)  279 us
    psum x1, waiting for transfers between devices, per_device(): sketch = lax.psum(local_sketch, 'col')  135 us
  transfers between devices with their start and end apart: 3, of which 3 were waited for; matrix products, arithmetic and copies ran while one was open for 1% of the time, Pallas kernels for 0%

commit v1 on v0

v1 whole, which is shorter than its diff:
```python
import functools

import jax
import jax.numpy as jnp
from jax import lax
from jax.experimental import pallas as pl
from jax.experimental.pallas import tpu as pltpu
from jax.sharding import PartitionSpec as P

PANEL = 512
STEPS = 2
NX = 4
NY = 4
LANE = 128
DELAY = 3
MESH = pl.DeviceIdType.MESH


def kernel(dims, ids, a_hbm, b_hbm, c_hbm, s_hbm, cout_hbm, sk_hbm, pr_hbm,
           a_v, bo_v, bp_v, c_v, s_v, sbuf, recv, precv, afull, bfull, cov,
           part, rsr, red, outb, bs, masks,
           bo_sem, bp_send, bp_recv, in_sem, send_sem, recv_sem, f_send, f_recv,
           rs_sem, out_sem):
    nz, ncol, nblk, total, rows_b, rows_k = dims
    seg = 2 * rows_b
    r = lax.axis_index("row")
    z = lax.axis_index("col")
    core = lax.rem(r, 2)
    chip = r // 2
    x = lax.rem(chip, NX)
    y = chip // NX

    def at_chip(yy, xx):
        return (lax.rem(yy + NY, NY) * NX + lax.rem(xx + NX, NX)) * 2 + core

    partner = (chip * 2 + (1 - core), z)
    links = (
        (at_chip(y, x + 1), z), (at_chip(y, x - 1), z),
        (at_chip(y + 1, x), z), (at_chip(y - 1, x), z),
        (r, lax.rem(z + 1, nz)), (r, lax.rem(z + nz - 1, nz)),
    )
    half = PANEL // 2
    mine = pl.multiple_of(core * half, half)
    other = pl.multiple_of((1 - core) * half, half)

    def own_load(j, k):
        rows = mine if j == 0 else other
        return pltpu.make_async_copy(
            b_hbm.at[pl.ds(rows, half), pl.ds(pl.multiple_of(k * LANE, LANE), LANE)],
            bo_v.at[k, pl.ds(rows, half), :], bo_sem.at[j, k])

    def partner_copy(j, k):
        rows = other if j == 0 else mine
        return pltpu.make_async_remote_copy(
            src_ref=b_hbm.at[pl.ds(rows, half), pl.ds(pl.multiple_of(k * LANE, LANE), LANE)],
            dst_ref=bp_v.at[k, pl.ds(rows, half), :],
            send_sem=bp_send.at[j, k], recv_sem=bp_recv.at[j, k],
            device_id=partner, device_id_type=MESH)

    load_a = pltpu.make_async_copy(a_hbm, a_v, in_sem.at[0])
    load_c = pltpu.make_async_copy(c_hbm, c_v, in_sem.at[1])
    load_s = pltpu.make_async_copy(s_hbm, s_v, in_sem.at[2])

    barrier = pltpu.get_barrier_semaphore()
    for target in links + (partner,):
        pl.semaphore_signal(barrier, inc=1, device_id=target, device_id_type=MESH)
    load_a.start()
    for k in range(nblk):
        own_load(0, k).start()
    pl.semaphore_wait(barrier, 7)
    for k in range(nblk):
        partner_copy(0, k).start()
    load_c.start()
    load_s.start()
    for k in range(nblk):
        own_load(1, k).start()
        partner_copy(1, k).start()
    load_a.wait()

    def flag(cond):
        return cond.astype(jnp.int32)

    def choose(cond, one, two):
        return two + cond * (one - two)

    def within(v, low, high):
        return flag(v >= low) * flag(v <= high)

    pid = [ids[s] for s in range(STEPS)]
    owner_core = [lax.rem(p, 2) for p in pid]
    ox = [lax.rem(lax.div(p, 2), NX) for p in pid]
    oy = [lax.div(p, 2 * NX) for p in pid]
    oz = [lax.div(p * PANEL, rows_k) for p in pid]
    oa = [lax.rem(p * PANEL, rows_k) for p in pid]
    dx = [lax.rem(x - o + NX, NX) for o in ox]
    dy = [lax.rem(y - o + NY, NY) for o in oy]
    for s in range(STEPS):
        flags = (
            flag(owner_core[s] == core),
            flag(dx[s] == 0) * flag(dy[s] == 0),
            within(dx[s], 1, NX - 2), within(dy[s], 1, NY - 2),
            within(dx[s], 2, NX - 1), within(dy[s], 2, NY - 1),
            flag(oz[s] == z),
            flag(oa[s] > 0),
        )
        for n, f in enumerate(flags):
            masks[s, n] = jnp.full((rows_b, LANE), f.astype(jnp.float32)).astype(jnp.bfloat16)
    here = [(s, 0) for s in range(STEPS)]
    root = [(s, 1) for s in range(STEPS)]
    xplus = [(s, 2) for s in range(STEPS)]
    yplus = [(s, 3) for s in range(STEPS)]
    xminus = [(s, 4) for s in range(STEPS)]
    yminus = [(s, 5) for s in range(STEPS)]
    zroot = [(s, 6) for s in range(STEPS)]

    def pick(where, one, two):
        return jnp.where(masks[where[0], where[1]] > 0, one, two)

    def own_b(s, k, base, q):
        rows = pl.ds(pl.multiple_of(base + q * rows_b, rows_b), rows_b)
        return pick(here[s], bo_v[k, rows, :], bp_v[k, rows, :])

    def own_a(s, k):
        f = k // (256 // rows_b)
        rb = lax.rem(k, 256 // rows_b)
        rows = pl.ds(pl.multiple_of(rb * rows_b, rows_b), rows_b)
        low = a_v[rows, pl.ds(pl.multiple_of(f * LANE, LANE), LANE)]
        high = a_v[rows, pl.ds(pl.multiple_of(PANEL + f * LANE, LANE), LANE)]
        return pick((s, 7), high, low)

    def message(t, link):
        return pltpu.make_async_remote_copy(
            src_ref=sbuf.at[t, link], dst_ref=recv.at[t, link],
            send_sem=send_sem.at[t], recv_sem=recv_sem.at[t],
            device_id=links[link], device_id_type=MESH)

    def forward(t):
        return pltpu.make_async_remote_copy(
            src_ref=recv.at[t, pl.ds(0, 4)], dst_ref=precv.at[t],
            send_sem=f_send.at[t], recv_sem=f_recv.at[t],
            device_id=partner, device_id_type=MESH)

    def wait_all(ref, sem):
        pltpu.make_async_copy(ref, ref, sem).wait()

    def stage(t, relay):
        kb = jnp.minimum(t, nblk - 1)
        ka = jnp.minimum(t, ncol - 1)
        for s in range(STEPS):
            rows = pl.ds(s * rows_b, rows_b)
            for link, q, keep in ((0, 0, xplus), (2, 2, yplus), (1, 1, xminus), (3, 3, yminus)):
                value = own_b(s, kb, mine, q)
                if relay:
                    mate = {0: 2, 2: 0, 1: 3, 3: 1}[link]
                    moved = pick(keep[s], recv[t - DELAY, link, rows, :], recv[t - DELAY, mate, rows, :])
                    value = pick(root[s], value, moved)
                sbuf[t, link, rows, :] = value
            for link in (4, 5):
                value = own_a(s, ka)
                if relay:
                    value = pick(zroot[s], value, recv[t - DELAY, link, rows, :])
                sbuf[t, link, rows, :] = value
        for link in range(6):
            message(t, link).start()

    for t in range(DELAY):
        own_load(0, t).wait()
        partner_copy(0, t).wait_recv()
        stage(t, False)

    def step(t, carry):
        wait_all(recv.at[t - DELAY], recv_sem.at[t - DELAY])
        forward(t - DELAY).start()

        @pl.when(t < nblk)
        def _():
            own_load(0, t).wait()
            partner_copy(0, t).wait_recv()

        stage(t, True)
        return carry

    lax.fori_loop(DELAY, total, step, 0)

    def last(t, carry):
        wait_all(recv.at[t], recv_sem.at[t])
        forward(t).start()
        return carry

    lax.fori_loop(total - DELAY, total, last, 0)

    for s in range(STEPS):
        hz = lax.rem(z - oz[s] + nz, nz)
        up = flag(hz <= nz // 2)
        hop = choose(up, hz, nz - hz)
        link = 5 - up
        first = (hop - 1 + flag(hop == 0)) * DELAY

        def take_a(k, carry, s=s, link=link, first=first):
            got = recv[k + first, link, pl.ds(s * rows_b, rows_b), :]
            value = pick(zroot[s], own_a(s, k), got)
            f = k // (256 // rows_b)
            rb = lax.rem(k, 256 // rows_b)
            afull[pl.ds(pl.multiple_of(rb * rows_b, rows_b), rows_b),
                  pl.ds(pl.multiple_of(s * PANEL + f * LANE, LANE), LANE)] = value
            return carry

        lax.fori_loop(0, ncol, take_a, 0)

    load_c.wait()
    load_s.wait()
    for k in range(nblk):
        own_load(1, k).wait()
        partner_copy(1, k).wait_recv()

    def settle(t, carry):
        f = forward(t)
        f.wait_recv()
        return carry

    lax.fori_loop(0, total, settle, 0)

    def where_from(s):
        out = []
        for sign, i, j in ((0, dx[s], dy[s]),
                           (1, lax.rem(NX - dx[s], NX), lax.rem(NY - dy[s], NY))):
            i0 = flag(i == 0)
            j0 = flag(j == 0)
            hx = i + j + NX * i0 * (1 - j0)
            hy = i + j + NY * j0 * (1 - i0)
            near = i0 + j0 - i0 * j0
            tx = (hx - 1 + i0 * j0) * DELAY
            ty = (hy - 1 + i0 * j0) * DELAY
            out.append((sign, choose(near, sign, 2 + sign), choose(near, tx, ty)))
            out.append((2 + sign, choose(near, 2 + sign, sign), choose(near, ty, tx)))
        return out

    routes = [where_from(s) for s in range(STEPS)]

    def take_b(k, carry):
        for s in range(STEPS):
            for q, link, first in routes[s]:
                for src, base in ((recv, mine), (precv, other)):
                    got = src[k + first, link, pl.ds(s * rows_b, rows_b), :]
                    value = pick(root[s], own_b(s, k, base, q), got)
                    bfull[pl.ds(pl.multiple_of(s * PANEL + base + q * rows_b, rows_b), rows_b),
                          pl.ds(pl.multiple_of(k * LANE, LANE), LANE)] = value
        return carry

    lax.fori_loop(0, nblk, take_b, 0)

    width = nblk * LANE
    sk = jnp.zeros((256, LANE), jnp.float32)
    bs[...] = jnp.zeros_like(bs)
    at = 0
    while at < width:
        w = min(256, width - at)
        cols = pl.ds(at, w)
        b_c = bfull[:, cols]
        acc = jnp.dot(afull[...], b_c, preferred_element_type=jnp.float32)
        c_new = (c_v[:, cols].astype(jnp.float32) + acc).astype(jnp.bfloat16)
        cov[:, cols] = c_new
        s_c = s_v[cols, :]
        sk = sk + jnp.dot(c_new, s_c, preferred_element_type=jnp.float32)
        bs[...] += jnp.dot(b_c, s_c, preferred_element_type=jnp.float32)
        at += w
    put_c = pltpu.make_async_copy(cov, cout_hbm, out_sem.at[0])
    put_c.start()
    part[0] = sk
    pr = jnp.zeros((256, LANE), jnp.float32)
    rest = bs[...]
    for _ in range(3):
        piece = rest.astype(jnp.bfloat16)
        pr = pr + jnp.dot(afull[...], piece, preferred_element_type=jnp.float32)
        rest = rest - piece.astype(jnp.float32)
    part[1] = pr

    nr = 256 // nz

    def rows_of(j):
        return pl.ds(pl.multiple_of(j * nr, nr), nr)

    order = sorted(range(1, nz), key=lambda d: -min(d, nz - d))

    def scatter(d):
        to = lax.rem(z + d, nz)
        return pltpu.make_async_remote_copy(
            src_ref=part.at[:, rows_of(to), :], dst_ref=rsr.at[d - 1],
            send_sem=rs_sem.at[0], recv_sem=rs_sem.at[1],
            device_id=(r, to), device_id_type=MESH)

    def gather(d):
        to = lax.rem(z + d, nz)
        return pltpu.make_async_remote_copy(
            src_ref=red, dst_ref=outb.at[:, rows_of(z), :],
            send_sem=rs_sem.at[2], recv_sem=rs_sem.at[3],
            device_id=(r, to), device_id_type=MESH)

    for d in order:
        scatter(d).start()
    wait_all(rsr, rs_sem.at[1])
    value = part[:, rows_of(z), :]
    for d in range(nz - 1):
        value = value + rsr[d]
    red[...] = value
    outb[:, rows_of(z), :] = value
    for d in order:
        gather(d).start()
    wait_all(rsr, rs_sem.at[3])
    put_s = pltpu.make_async_copy(outb.at[0], sk_hbm, out_sem.at[1])
    put_p = pltpu.make_async_copy(outb.at[1], pr_hbm, out_sem.at[2])
    put_s.start()
    put_p.start()

    wait_all(rsr, rs_sem.at[0])
    wait_all(rsr, rs_sem.at[2])

    def drain(t, carry):
        wait_all(sbuf.at[t], send_sem.at[t])
        forward(t).wait_send()
        return carry

    lax.fori_loop(0, total, drain, 0)
    for k in range(nblk):
        for j in range(2):
            partner_copy(j, k).wait_send()
    put_c.wait()
    put_s.wait()
    put_p.wait()


def per_device(nz, a_tile, b_tile, c_prior, sketch_matrix, panel_ids):
    rows_b = 64
    seg = 2 * rows_b
    width = b_tile.shape[1]
    nblk = width // LANE
    rows_k = a_tile.shape[1]
    ncol = (PANEL // LANE) * (256 // rows_b)
    total = max(nblk + 6 * DELAY, ncol + (nz // 2 - 1) * DELAY)
    bf = jnp.bfloat16
    f32 = jnp.float32
    dma = pltpu.SemaphoreType.DMA
    dims = (nz, ncol, nblk, total, rows_b, rows_k)
    hbm = pl.BlockSpec(memory_space=pl.ANY)
    return pl.pallas_call(
        functools.partial(kernel, dims),
        out_shape=(
            jax.ShapeDtypeStruct((256, width), bf),
            jax.ShapeDtypeStruct((256, LANE), f32),
            jax.ShapeDtypeStruct((256, LANE), f32),
        ),
        in_specs=[pl.BlockSpec(memory_space=pltpu.SMEM)] + [hbm] * 4,
        out_specs=(hbm,) * 3,
        scratch_shapes=[
            pltpu.VMEM((256, rows_k), bf),
            pltpu.VMEM((nblk, PANEL, LANE), bf),
            pltpu.VMEM((nblk, PANEL, LANE), bf),
            pltpu.VMEM((256, width), bf),
            pltpu.VMEM((width, LANE), bf),
            pltpu.VMEM((total, 6, seg, LANE), bf),
            pltpu.VMEM((total, 6, seg, LANE), bf),
            pltpu.VMEM((total, 4, seg, LANE), bf),
            pltpu.VMEM((256, STEPS * PANEL), bf),
            pltpu.VMEM((STEPS * PANEL, width), bf),
            pltpu.VMEM((256, width), bf),
            pltpu.VMEM((2, 256, LANE), f32),
            pltpu.VMEM((nz - 1, 2, 256 // nz, LANE), f32),
            pltpu.VMEM((2, 256 // nz, LANE), f32),
            pltpu.VMEM((2, 256, LANE), f32),
            pltpu.VMEM((STEPS * PANEL, LANE), f32),
            pltpu.VMEM((STEPS, 8, rows_b, LANE), bf),
            dma((2, nblk)), dma((2, nblk)), dma((2, nblk)), dma((3,)),
            dma((total,)), dma((total,)), dma((total,)), dma((total,)),
            dma((4,)), dma((3,)),
        ],
        compiler_params=pltpu.CompilerParams(
            collective_id=0, has_side_effects=True, vmem_limit_bytes=60 * 1024 * 1024),
    )(panel_ids, a_tile, b_tile, c_prior, sketch_matrix)


def solution(mesh):
    placed = (P("row", "col"), P("row", "col"), P("row", "col"), P("col", None), P())
    return jax.shard_map(
        functools.partial(per_device, mesh.shape["col"]),
        mesh=mesh,
        in_specs=placed,
        out_specs=(P("row", "col"), P("row", None), P("row", None)),
        check_vma=False,
    )
```

time: 450 us -> 104 us (0.23)
  the two profiles are of different devices: /device:TPU:2 before, /device:TPU:1 now
where the time goes in v1:
time: 104 us; the launch traced here: 103 us
  Pallas kernels  99.1 us (95%)
  local copies, waits for them, and re-layouts  3.48 us (3%)
    pallas_call x1, Pallas kernels, per_device(): pl.pallas_call(functools.partial(kernel, dims), out_shape=(jax.ShapeDtype...  99.1 us
    unnamed x7, local copies, waits for them, and re-layouts  3.48 us

profile of v1, /device:TPU:1, one launch (start us, length us, event | category | flops | bytes accessed | tf_op | source)
XLA Modules:
  0.0 103.3 jit_solution(18192731300300233378)
XLA Ops:
  0.6 99.1 %shard_map.76 = (bf16[256,1664]{1,0:T(8,128)(2,1)}, f32[256,128]{1,0:T(8,128)}, f32[256,128]{1,0:T(8,128)}) custom-call(s32[2]{0:T(128)} %ids.1, bf16[256,1024]{1,0:T(8,128)(2,1)} %a_hbm.1, bf16[512,1664]{1,0:T(8,128)(2,1)} %b_hbm.1, bf16[256,1664]{1,0:T(8,128)(2,1)} %c_hbm.1, bf16[1664,128]{1,0:T(8,128)(2,1)} %s_hbm.1), custom_call_target="tpu_custom_call" | custom-call | tf_op jit(solution)/shard_map/pallas_call | solution.py:345
  99.8 0.0 copy-start.1
  99.8 0.0 copy-start
  99.8 2.2 %copy.11 = bf16[256,1664]{1,0:T(8,128)(2,1)} copy(bf16[256,1664]{1,0:T(8,128)(2,1)} %get-tuple-element.6) | data formatting | bytes 1703936
  101.9 0.0 copy-done.1
  101.9 0.7 copy.12
  102.6 0.0 copy-done
  102.6 0.7 copy.13
Async XLA Ops:
  99.8 2.2 %copy-start.1 = (f32[256,128]{1,0:T(8,128)S(1)}, f32[256,128]{1,0:T(8,128)}, u32[]{:S(2)}) copy-start(f32[256,128]{1,0:T(8,128)} %get-tuple-element.7) | copy-start | bytes 393220
  99.8 2.8 %copy-start = (f32[256,128]{1,0:T(8,128)S(1)}, f32[256,128]{1,0:T(8,128)}, u32[]{:S(2)}) copy-start(f32[256,128]{1,0:T(8,128)} %get-tuple-element.8) | copy-start | bytes 393220

commit v2 on v0

v2 whole, which is shorter than its diff:
```python
import functools

import jax
import jax.numpy as jnp
from jax import lax
from jax.experimental import pallas as pl
from jax.experimental.pallas import tpu as pltpu
from jax.sharding import PartitionSpec as P

PANEL = 512
STEPS = 2
NX = 4
NY = 4
LANE = 128
PART = 128
DELAY_A = 4
DELAY_B = 5
PIECES = ((0, 2), (2, 6), (6, 13))
MESH = pl.DeviceIdType.MESH


def kernel(dims, ids, a_hbm, b_hbm, c_hbm, s_hbm, cout_hbm, sk_hbm, pr_hbm,
           ab_v, bo_v, bp_v, c_v, s_v, sb, sa, rb, ra, afull, bfull, cov,
           part, rsr, red, outb, bs, masks,
           in_sem, bo_sem, bp_send, bp_recv, ap_sem,
           sb_sem, rb_sem, sa_sem, ra_sem, fb_send, fb_recv, fa_send, fa_recv,
           rs_sem, out_sem):
    nz, na, nb, ta, tb, rows_k = dims
    r = lax.axis_index("row")
    z = lax.axis_index("col")
    core = lax.rem(r, 2)
    chip = r // 2
    x = lax.rem(chip, NX)
    y = chip // NX
    first_core = core == 0
    second_core = core == 1

    def at_chip(yy, xx):
        return (lax.rem(yy + NY, NY) * NX + lax.rem(xx + NX, NX)) * 2 + core

    partner = (chip * 2 + (1 - core), z)
    plane = ((at_chip(y, x + 1), z), (at_chip(y, x - 1), z),
             (at_chip(y + 1, x), z), (at_chip(y - 1, x), z))
    line = ((r, lax.rem(z + 1, nz)), (r, lax.rem(z + nz - 1, nz)))

    def piece(j):
        low, high = PIECES[j]
        return pl.ds(low * LANE, (high - low) * LANE)

    def own_load(j):
        return pltpu.make_async_copy(b_hbm.at[:, piece(j)], bo_v.at[:, piece(j)], bo_sem.at[j])

    def partner_copy(j):
        return pltpu.make_async_remote_copy(
            src_ref=bo_v.at[:, piece(j)], dst_ref=bp_v.at[:, piece(j)],
            send_sem=bp_send.at[j], recv_sem=bp_recv.at[j],
            device_id=partner, device_id_type=MESH)

    load_a = pltpu.make_async_copy(a_hbm, ab_v.at[core], in_sem.at[0])
    load_c = pltpu.make_async_copy(c_hbm, c_v, in_sem.at[1])
    load_s = pltpu.make_async_copy(s_hbm, s_v, in_sem.at[2])
    partner_a = pltpu.make_async_remote_copy(
        src_ref=ab_v.at[0], dst_ref=ab_v.at[0], send_sem=ap_sem.at[0], recv_sem=ap_sem.at[1],
        device_id=partner, device_id_type=MESH)
    npc = len(PIECES)

    barrier = pltpu.get_barrier_semaphore()
    pl.semaphore_signal(barrier, inc=1, device_id=partner, device_id_type=MESH)

    @pl.when(first_core)
    def _():
        for target in plane:
            pl.semaphore_signal(barrier, inc=1, device_id=target, device_id_type=MESH)

    @pl.when(second_core)
    def _():
        for target in line:
            pl.semaphore_signal(barrier, inc=1, device_id=target, device_id_type=MESH)

    load_a.start()
    for j in range(npc):
        own_load(j).start()

    def flag(cond):
        return cond.astype(jnp.int32)

    def choose(cond, one, two):
        return two + cond * (one - two)

    def within(v, low, high):
        return flag(v >= low) * flag(v <= high)

    pid = [ids[s] for s in range(STEPS)]
    owner_core = [lax.rem(p, 2) for p in pid]
    ox = [lax.rem(lax.div(p, 2), NX) for p in pid]
    oy = [lax.div(p, 2 * NX) for p in pid]
    oz = [lax.div(p * PANEL, rows_k) for p in pid]
    oa = [lax.rem(p * PANEL, rows_k) for p in pid]
    dx = [[lax.rem(g * (x - o) + NX, NX) for o in ox] for g in (1, -1)]
    dy = [[lax.rem(g * (y - o) + NY, NY) for o in oy] for g in (1, -1)]
    for s in range(STEPS):
        flags = (
            flag(owner_core[s] == core), flag(dx[0][s] == 0) * flag(dy[0][s] == 0),
            within(dx[0][s], 1, NX - 2), within(dx[1][s], 1, NX - 2),
            within(dy[0][s], 1, NY - 2), within(dy[1][s], 1, NY - 2),
            flag(oz[s] == z), flag(oa[s] > 0),
        )
        for n, f in enumerate(flags):
            masks[s, n] = jnp.full((PART, LANE), f.astype(jnp.float32)).astype(jnp.bfloat16)
    HERE, ROOT, KEEP, ZROOT, HIGH = 0, 1, 2, 6, 7

    def pick(s, n, one, two):
        return jnp.where(masks[s, n] > 0, one, two)

    def lanes(k):
        return pl.ds(pl.multiple_of(k * LANE, LANE), LANE)

    def own_b(s, k, base):
        rows = pl.ds(pl.multiple_of(base, PART), PART)
        return pick(s, HERE, bo_v[rows, lanes(k)], bp_v[rows, lanes(k)])

    def own_a(s, f, tile, j):
        rows = pl.ds(pl.multiple_of(j * PART, PART), PART)
        return pick(s, HIGH, ab_v[tile, rows, lanes(PANEL // LANE + f)], ab_v[tile, rows, lanes(f)])

    def send_b(t, link):
        return pltpu.make_async_remote_copy(
            src_ref=sb.at[t, link], dst_ref=rb.at[t, link],
            send_sem=sb_sem.at[t], recv_sem=rb_sem.at[t],
            device_id=plane[link], device_id_type=MESH)

    def send_a(t, link, src):
        return pltpu.make_async_remote_copy(
            src_ref=src, dst_ref=ra.at[t, link],
            send_sem=sa_sem.at[t], recv_sem=ra_sem.at[t],
            device_id=line[link], device_id_type=MESH)

    def share_b(t):
        return pltpu.make_async_remote_copy(
            src_ref=rb.at[t], dst_ref=rb.at[t],
            send_sem=fb_send.at[t], recv_sem=fb_recv.at[t],
            device_id=partner, device_id_type=MESH)

    def share_a(t):
        return pltpu.make_async_remote_copy(
            src_ref=ra.at[t], dst_ref=ra.at[t],
            send_sem=fa_send.at[t], recv_sem=fa_recv.at[t],
            device_id=partner, device_id_type=MESH)

    def wait_all(ref, sem):
        pltpu.make_async_copy(ref, ref, sem).wait()

    def stage_b(t, own, relay):
        for link, sign in ((0, 0), (1, 1), (2, 0), (3, 1)):
            mate = (link + 2) % 4
            q = link // 2
            for s in range(STEPS):
                rows = pl.ds(s * PART, PART)
                value = None
                if relay:
                    value = pick(s, KEEP + link, rb[t - DELAY_B, link, rows, :],
                                 rb[t - DELAY_B, mate, rows, :])
                if own:
                    mine = own_b(s, t, sign * (PANEL // 2) + q * PART)
                    value = pick(s, ROOT, mine, value) if relay else mine
                sb[t, link, rows, :] = value
            send_b(t, link).start()

    def stage_a(t, relay):
        for s in range(STEPS):
            rows = pl.ds(s * PART, PART)
            value = own_a(s, t // 4, lax.rem(t, 4) // 2, lax.rem(t, 2))
            for link in range(2):
                sa[t, link, rows, :] = (
                    pick(s, ZROOT, value, ra[t - DELAY_A, link, rows, :]) if relay else value)
        for link in range(2):
            send_a(t, link, sa.at[t, link]).start()

    @pl.when(first_core)
    def _():
        load_a.wait()
        pl.semaphore_wait(barrier, 5)
        partner_a.start()
        for t in range(DELAY_B):
            for j, (low, _) in enumerate(PIECES):
                if low == t:
                    own_load(j).wait()
                    partner_copy(j).start()
                    partner_copy(j).wait_recv()
            stage_b(t, True, False)
        load_c.start()
        load_s.start()

        def begin(t, carry):
            for j, (low, _) in enumerate(PIECES):
                if low >= DELAY_B:
                    @pl.when(t == low)
                    def _(j=j):
                        own_load(j).wait()
                        partner_copy(j).start()
                        partner_copy(j).wait_recv()

            wait_all(rb.at[t - DELAY_B], rb_sem.at[t - DELAY_B])
            stage_b(t, True, True)
            share_b(t - DELAY_B).start()
            return carry

        def relay(t, carry):
            wait_all(rb.at[t - DELAY_B], rb_sem.at[t - DELAY_B])
            stage_b(t, False, True)
            share_b(t - DELAY_B).start()
            return carry

        def last(t, carry):
            wait_all(rb.at[t], rb_sem.at[t])
            share_b(t).start()
            return carry

        lax.fori_loop(DELAY_B, nb, begin, 0)
        lax.fori_loop(nb, tb, relay, 0)
        lax.fori_loop(tb - DELAY_B, tb, last, 0)

    @pl.when(second_core)
    def _():
        pl.semaphore_wait(barrier, 3)
        for j in range(npc):
            own_load(j).wait()
            partner_copy(j).start()
        load_a.wait()
        partner_a.wait_recv()
        for t in range(DELAY_A):
            stage_a(t, False)
        load_c.start()
        load_s.start()

        def begin(t, carry):
            wait_all(ra.at[t - DELAY_A], ra_sem.at[t - DELAY_A])
            stage_a(t, True)
            share_a(t - DELAY_A).start()
            return carry

        def relay(t, carry):
            wait_all(ra.at[t - DELAY_A], ra_sem.at[t - DELAY_A])
            for link in range(2):
                send_a(t, link, ra.at[t - DELAY_A, link]).start()
            share_a(t - DELAY_A).start()
            return carry

        def last(t, carry):
            wait_all(ra.at[t], ra_sem.at[t])
            share_a(t).start()
            return carry

        lax.fori_loop(DELAY_A, na, begin, 0)
        lax.fori_loop(na, ta, relay, 0)
        lax.fori_loop(ta - DELAY_A, ta, last, 0)
        for j in range(npc):
            partner_copy(j).wait_recv()

        def settle(t, carry):
            wait_all(rb.at[t], fb_recv.at[t])
            return carry

        lax.fori_loop(0, tb, settle, 0)

    load_c.wait()
    load_s.wait()

    routes = []
    for s in range(STEPS):
        for g in range(2):
            i, j = dx[g][s], dy[g][s]
            i0, j0 = flag(i == 0), flag(j == 0)
            near = i0 + j0 - i0 * j0
            tx = (i + j + NX * i0 * (1 - j0) - 1 + i0 * j0) * DELAY_B
            ty = (i + j + NY * j0 * (1 - i0) - 1 + i0 * j0) * DELAY_B
            routes.append((s, g, 0, g + 2 * (1 - near), choose(near, tx, ty)))
            routes.append((s, g, 1, g + 2 * near, choose(near, ty, tx)))

    def take_b(k, carry):
        for s, g, q, link, first in routes:
            base = g * (PANEL // 2) + q * PART
            got = rb[k + first, link, pl.ds(s * PART, PART), :]
            bfull[pl.ds(s * PANEL + base, PART), lanes(k)] = pick(s, ROOT, own_b(s, k, base), got)
        return carry

    lax.fori_loop(0, nb, take_b, 0)

    width = nb * LANE
    blocks = [pl.ds(at, min(256, width - at)) for at in range(0, width, 256)]
    bs[...] = jnp.zeros_like(bs)
    for cols in blocks:
        bs[...] += jnp.dot(bfull[:, cols], s_v[cols, :], preferred_element_type=jnp.float32)

    @pl.when(first_core)
    def _():
        def settle(t, carry):
            wait_all(ra.at[t], fa_recv.at[t])
            return carry

        lax.fori_loop(0, ta, settle, 0)

    for s in range(STEPS):
        hz = lax.rem(z - oz[s] + nz, nz)
        down = flag(hz > nz // 2)
        hop = choose(down, nz - hz, hz)
        first = (hop - 1 + flag(hop == 0)) * DELAY_A
        for f in range(PANEL // LANE):
            for j in range(2):
                got = ra[first + 4 * f + 2 * core + j, down, pl.ds(s * PART, PART), :]
                afull[pl.ds(j * PART, PART), pl.ds(s * PANEL + f * LANE, LANE)] = pick(
                    s, ZROOT, own_a(s, f, core, j), got)

    nr = 256 // nz

    def rows_of(j):
        return pl.ds(pl.multiple_of(j * nr, nr), nr)

    order = sorted(range(1, nz), key=lambda d: -min(d, nz - d))

    def scatter(n, d):
        to = lax.rem(z + d, nz)
        return pltpu.make_async_remote_copy(
            src_ref=part.at[n, rows_of(to), :], dst_ref=rsr.at[n, d - 1],
            send_sem=rs_sem.at[n, 0], recv_sem=rs_sem.at[n, 1],
            device_id=(r, to), device_id_type=MESH)

    def gather(n, d):
        to = lax.rem(z + d, nz)
        return pltpu.make_async_remote_copy(
            src_ref=red.at[n], dst_ref=outb.at[n, rows_of(z), :],
            send_sem=rs_sem.at[n, 2], recv_sem=rs_sem.at[n, 3],
            device_id=(r, to), device_id_type=MESH)

    def reduce(n):
        wait_all(rsr.at[n], rs_sem.at[n, 1])
        value = part[n, rows_of(z), :]
        for d in range(nz - 1):
            value = value + rsr[n, d]
        red[n] = value
        outb[n, rows_of(z), :] = value
        for d in order:
            gather(n, d).start()

    pr = jnp.zeros((256, LANE), jnp.float32)
    rest = bs[...]
    for _ in range(3):
        term = rest.astype(jnp.bfloat16)
        pr = pr + jnp.dot(afull[...], term, preferred_element_type=jnp.float32)
        rest = rest - term.astype(jnp.float32)
    part[1] = pr
    for d in order:
        scatter(1, d).start()
    sk = jnp.zeros((256, LANE), jnp.float32)
    for cols in blocks:
        acc = jnp.dot(afull[...], bfull[:, cols], preferred_element_type=jnp.float32)
        c_new = (c_v[:, cols].astype(jnp.float32) + acc).astype(jnp.bfloat16)
        cov[:, cols] = c_new
        sk = sk + jnp.dot(c_new, s_v[cols, :], preferred_element_type=jnp.float32)
    part[0] = sk
    for d in order:
        scatter(0, d).start()
    put_c = pltpu.make_async_copy(cov, cout_hbm, out_sem.at[0])
    put_c.start()
    reduce(1)
    reduce(0)

    @pl.when(first_core)
    def _():
        def drain(t, carry):
            wait_all(sb.at[t], sb_sem.at[t])
            share_b(t).wait_send()
            return carry

        lax.fori_loop(0, tb, drain, 0)
        partner_a.wait_send()

    @pl.when(second_core)
    def _():
        def drain(t, carry):
            wait_all(sa.at[0], sa_sem.at[t])
            share_a(t).wait_send()
            return carry

        lax.fori_loop(0, ta, drain, 0)

    for j in range(npc):
        partner_copy(j).wait_send()
    wait_all(rsr.at[1], rs_sem.at[1, 0])
    wait_all(rsr.at[0], rs_sem.at[0, 0])
    wait_all(rsr.at[1], rs_sem.at[1, 2])
    put_c.wait()
    wait_all(rsr.at[1], rs_sem.at[1, 3])
    put_p = pltpu.make_async_copy(outb.at[1], pr_hbm, out_sem.at[2])
    put_p.start()
    wait_all(rsr.at[0], rs_sem.at[0, 3])
    put_s = pltpu.make_async_copy(outb.at[0], sk_hbm, out_sem.at[1])
    put_s.start()
    wait_all(rsr.at[0], rs_sem.at[0, 2])
    put_s.wait()
    put_p.wait()


def per_device(nz, a_tile, b_tile, c_prior, sketch_matrix, panel_ids):
    width = b_tile.shape[1]
    nb = width // LANE
    rows_k = a_tile.shape[1]
    na = (PANEL // LANE) * (2 * 256 // PART)
    tb = nb + 6 * DELAY_B
    ta = na + (nz // 2 - 1) * DELAY_A
    bf = jnp.bfloat16
    f32 = jnp.float32
    dma = pltpu.SemaphoreType.DMA
    vmem = pltpu.VMEM
    nr = 256 // nz
    npc = len(PIECES)
    hbm = pl.BlockSpec(memory_space=pl.ANY)
    return pl.pallas_call(
        functools.partial(kernel, (nz, na, nb, ta, tb, rows_k)),
        out_shape=(
            jax.ShapeDtypeStruct((256, width), bf),
            jax.ShapeDtypeStruct((256, LANE), f32),
            jax.ShapeDtypeStruct((256, LANE), f32),
        ),
        in_specs=[pl.BlockSpec(memory_space=pltpu.SMEM)] + [hbm] * 4,
        out_specs=(hbm,) * 3,
        scratch_shapes=[
            vmem((2, 256, rows_k), bf),
            vmem((PANEL, width), bf),
            vmem((PANEL, width), bf),
            vmem((256, width), bf),
            vmem((width, LANE), bf),
            vmem((tb, 4, STEPS * PART, LANE), bf),
            vmem((na, 2, STEPS * PART, LANE), bf),
            vmem((tb, 4, STEPS * PART, LANE), bf),
            vmem((ta, 2, STEPS * PART, LANE), bf),
            vmem((256, STEPS * PANEL), bf),
            vmem((STEPS * PANEL, width), bf),
            vmem((256, width), bf),
            vmem((2, 256, LANE), f32),
            vmem((2, nz - 1, nr, LANE), f32),
            vmem((2, nr, LANE), f32),
            vmem((2, 256, LANE), f32),
            vmem((STEPS * PANEL, LANE), f32),
            vmem((STEPS, 8, PART, LANE), bf),
            dma((3,)), dma((npc,)), dma((npc,)), dma((npc,)), dma((2,)),
            dma((tb,)), dma((tb,)), dma((ta,)), dma((ta,)),
            dma((tb,)), dma((tb,)), dma((ta,)), dma((ta,)),
            dma((2, 4)), dma((3,)),
        ],
        compiler_params=pltpu.CompilerParams(
            collective_id=0, has_side_effects=True, vmem_limit_bytes=60 * 1024 * 1024),
    )(panel_ids, a_tile, b_tile, c_prior, sketch_matrix)


def solution(mesh):
    placed = (P("row", "col"), P("row", "col"), P("row", "col"), P("col", None), P())
    return jax.shard_map(
        functools.partial(per_device, mesh.shape["col"]),
        mesh=mesh,
        in_specs=placed,
        out_specs=(P("row", "col"), P("row", None), P("row", None)),
        check_vma=False,
    )
```

time: 450 us -> 91.7 us (0.20)
  the two profiles are of different devices: /device:TPU:2 before, /device:TPU:1 now
where the time goes in v2:
time: 91.7 us; the launch traced here: 91.5 us
  Pallas kernels  87.4 us (95%)
  local copies, waits for them, and re-layouts  3.48 us (4%)
    pallas_call x1, Pallas kernels, per_device(): pl.pallas_call(functools.partial(kernel, (nz, na, nb, ta, tb, rows_k)), o...  87.4 us
    unnamed x7, local copies, waits for them, and re-layouts  3.48 us

profile of v2, /device:TPU:1, one launch (start us, length us, event | category | flops | bytes accessed | tf_op | source)
XLA Modules:
  0.0 91.5 jit_solution(1699041672729012161)
XLA Ops:
  0.6 87.4 %shard_map.76 = (bf16[256,1664]{1,0:T(8,128)(2,1)}, f32[256,128]{1,0:T(8,128)}, f32[256,128]{1,0:T(8,128)}) custom-call(s32[2]{0:T(128)} %ids.1, bf16[256,1024]{1,0:T(8,128)(2,1)} %a_hbm.1, bf16[512,1664]{1,0:T(8,128)(2,1)} %b_hbm.1, bf16[256,1664]{1,0:T(8,128)(2,1)} %c_hbm.1, bf16[1664,128]{1,0:T(8,128)(2,1)} %s_hbm.1), custom_call_target="tpu_custom_call" | custom-call | tf_op jit(solution)/shard_map/pallas_call | solution.py:418
  88.0 0.0 copy-start.1
  88.0 0.0 copy-start
  88.1 2.2 %copy.11 = bf16[256,1664]{1,0:T(8,128)(2,1)} copy(bf16[256,1664]{1,0:T(8,128)(2,1)} %get-tuple-element.6) | data formatting | bytes 1703936
  90.2 0.0 copy-done.1
  90.2 0.7 copy.12
  90.9 0.0 copy-done
  90.9 0.7 copy.13
Async XLA Ops:
  88.0 2.2 %copy-start.1 = (f32[256,128]{1,0:T(8,128)S(1)}, f32[256,128]{1,0:T(8,128)}, u32[]{:S(2)}) copy-start(f32[256,128]{1,0:T(8,128)} %get-tuple-element.7) | copy-start | bytes 393220
  88.0 2.8 %copy-start = (f32[256,128]{1,0:T(8,128)S(1)}, f32[256,128]{1,0:T(8,128)}, u32[]{:S(2)}) copy-start(f32[256,128]{1,0:T(8,128)} %get-tuple-element.8) | copy-start | bytes 393220

commit v3 on v2

--- a/solution.py
+++ b/solution.py
@@ -13,6 +13,7 @@
 NY = 4
 LANE = 128
 PART = 128
+TILE = 16
 DELAY_A = 4
 DELAY_B = 5
 PIECES = ((0, 2), (2, 6), (6, 13))
@@ -21,7 +22,7 @@
 
 def kernel(dims, ids, a_hbm, b_hbm, c_hbm, s_hbm, cout_hbm, sk_hbm, pr_hbm,
            ab_v, bo_v, bp_v, c_v, s_v, sb, sa, rb, ra, afull, bfull, cov,
-           part, rsr, red, outb, bs, masks,
+           part, rsr, red, outg, outb, bs, masks,
            in_sem, bo_sem, bp_send, bp_recv, ap_sem,
            sb_sem, rb_sem, sa_sem, ra_sem, fb_send, fb_recv, fa_send, fa_recv,
            rs_sem, out_sem):
@@ -106,11 +107,12 @@
             flag(oz[s] == z), flag(oa[s] > 0),
         )
         for n, f in enumerate(flags):
-            masks[s, n] = jnp.full((PART, LANE), f.astype(jnp.float32)).astype(jnp.bfloat16)
+            masks[s, n] = jnp.full((TILE, LANE), f.astype(jnp.float32)).astype(jnp.bfloat16)
     HERE, ROOT, KEEP, ZROOT, HIGH = 0, 1, 2, 6, 7
 
     def pick(s, n, one, two):
-        return jnp.where(masks[s, n] > 0, one, two)
+        keep = jnp.concatenate([masks[s, n]] * (PART // TILE), axis=0) > 0
+        return jnp.where(keep, one, two)
 
     def lanes(k):
         return pl.ds(pl.multiple_of(k * LANE, LANE), LANE)
@@ -328,7 +330,7 @@
     def gather(n, d):
         to = lax.rem(z + d, nz)
         return pltpu.make_async_remote_copy(
-            src_ref=red.at[n], dst_ref=outb.at[n, rows_of(z), :],
+            src_ref=red.at[n], dst_ref=outg.at[n, rows_of(z), :],
             send_sem=rs_sem.at[n, 2], recv_sem=rs_sem.at[n, 3],
             device_id=(r, to), device_id_type=MESH)
 
@@ -337,8 +339,8 @@
         value = part[n, rows_of(z), :]
         for d in range(nz - 1):
             value = value + rsr[n, d]
-        red[n] = value
-        outb[n, rows_of(z), :] = value
+        red[n] = value.astype(jnp.bfloat16)
+        outg[n, rows_of(z), :] = value.astype(jnp.bfloat16)
         for d in order:
             gather(n, d).start()
 
@@ -388,15 +390,18 @@
         partner_copy(j).wait_send()
     wait_all(rsr.at[1], rs_sem.at[1, 0])
     wait_all(rsr.at[0], rs_sem.at[0, 0])
-    wait_all(rsr.at[1], rs_sem.at[1, 2])
+    others = pl.ds(0, 256 - nr)
+    wait_all(outg.at[1, others], rs_sem.at[1, 2])
     put_c.wait()
-    wait_all(rsr.at[1], rs_sem.at[1, 3])
+    wait_all(outg.at[1, others], rs_sem.at[1, 3])
+    outb[1] = outg[1].astype(jnp.float32)
     put_p = pltpu.make_async_copy(outb.at[1], pr_hbm, out_sem.at[2])
     put_p.start()
-    wait_all(rsr.at[0], rs_sem.at[0, 3])
+    wait_all(outg.at[0, others], rs_sem.at[0, 3])
+    outb[0] = outg[0].astype(jnp.float32)
     put_s = pltpu.make_async_copy(outb.at[0], sk_hbm, out_sem.at[1])
     put_s.start()
-    wait_all(rsr.at[0], rs_sem.at[0, 2])
+    wait_all(outg.at[0, others], rs_sem.at[0, 2])
     put_s.wait()
     put_p.wait()
 
@@ -439,10 +444,11 @@
             vmem((256, width), bf),
             vmem((2, 256, LANE), f32),
             vmem((2, nz - 1, nr, LANE), f32),
-            vmem((2, nr, LANE), f32),
+            vmem((2, nr, LANE), bf),
+            vmem((2, 256, LANE), bf),
             vmem((2, 256, LANE), f32),
             vmem((STEPS * PANEL, LANE), f32),
-            vmem((STEPS, 8, PART, LANE), bf),
+            vmem((STEPS, 8, TILE, LANE), bf),
             dma((3,)), dma((npc,)), dma((npc,)), dma((npc,)), dma((2,)),
             dma((tb,)), dma((tb,)), dma((ta,)), dma((ta,)),
             dma((tb,)), dma((tb,)), dma((ta,)), dma((ta,)),

time: 91.7 us -> 85.9 us (0.937)
  Pallas kernels: 87.4 us -> 81.6 us
    pallas_call x1, Pallas kernels: 87.4 us -> 81.6 us  [per_device(): pl.pallas_call(functools.partial(kernel, (nz, na, nb, ta, tb, rows_k)), o...]
where the time goes in v3:
time: 85.9 us; the launch traced here: 85.7 us
  Pallas kernels  81.6 us (95%)
  local copies, waits for them, and re-layouts  3.48 us (4%)
    pallas_call x1, Pallas kernels, per_device(): pl.pallas_call(functools.partial(kernel, (nz, na, nb, ta, tb, rows_k)), o...  81.6 us
    unnamed x7, local copies, waits for them, and re-layouts  3.48 us

profile of v3, /device:TPU:1, one launch (start us, length us, event | category | flops | bytes accessed | tf_op | source)
XLA Modules:
  0.0 85.7 jit_solution(1147685634003141728)
XLA Ops:
  0.6 81.6 %shard_map.76 = (bf16[256,1664]{1,0:T(8,128)(2,1)}, f32[256,128]{1,0:T(8,128)}, f32[256,128]{1,0:T(8,128)}) custom-call(s32[2]{0:T(128)} %ids.1, bf16[256,1024]{1,0:T(8,128)(2,1)} %a_hbm.1, bf16[512,1664]{1,0:T(8,128)(2,1)} %b_hbm.1, bf16[256,1664]{1,0:T(8,128)(2,1)} %c_hbm.1, bf16[1664,128]{1,0:T(8,128)(2,1)} %s_hbm.1), custom_call_target="tpu_custom_call" | custom-call | tf_op jit(solution)/shard_map/pallas_call | solution.py:423
  82.2 0.0 copy-start.1
  82.2 0.0 copy-start
  82.3 2.2 %copy.11 = bf16[256,1664]{1,0:T(8,128)(2,1)} copy(bf16[256,1664]{1,0:T(8,128)(2,1)} %get-tuple-element.6) | data formatting | bytes 1703936
  84.4 0.0 copy-done.1
  84.4 0.7 copy.12
  85.1 0.0 copy-done
  85.1 0.7 copy.13
Async XLA Ops:
  82.2 2.2 %copy-start.1 = (f32[256,128]{1,0:T(8,128)S(1)}, f32[256,128]{1,0:T(8,128)}, u32[]{:S(2)}) copy-start(f32[256,128]{1,0:T(8,128)} %get-tuple-element.7) | copy-start | bytes 393220
  82.2 2.8 %copy-start = (f32[256,128]{1,0:T(8,128)S(1)}, f32[256,128]{1,0:T(8,128)}, u32[]{:S(2)}) copy-start(f32[256,128]{1,0:T(8,128)} %get-tuple-element.8) | copy-start | bytes 393220

commit v4 on v3

--- a/solution.py
+++ b/solution.py
@@ -406,6 +406,19 @@
     put_p.wait()
 
 
+def finish(*refs):
+    ins, outs, held, sems = refs[:3], refs[3:6], refs[6:9], refs[9]
+    loads = [pltpu.make_async_copy(i, h, sems.at[0, n]) for n, (i, h) in enumerate(zip(ins, held))]
+    stores = [pltpu.make_async_copy(h, o, sems.at[1, n]) for n, (h, o) in enumerate(zip(held, outs))]
+    for load in loads:
+        load.start()
+    for load, store in zip(loads, stores):
+        load.wait()
+        store.start()
+    for store in stores:
+        store.wait()
+
+
 def per_device(nz, a_tile, b_tile, c_prior, sketch_matrix, panel_ids):
     width = b_tile.shape[1]
     nb = width // LANE
@@ -420,7 +433,7 @@
     nr = 256 // nz
     npc = len(PIECES)
     hbm = pl.BlockSpec(memory_space=pl.ANY)
-    return pl.pallas_call(
+    results = pl.pallas_call(
         functools.partial(kernel, (nz, na, nb, ta, tb, rows_k)),
         out_shape=(
             jax.ShapeDtypeStruct((256, width), bf),
@@ -457,6 +470,13 @@
         compiler_params=pltpu.CompilerParams(
             collective_id=0, has_side_effects=True, vmem_limit_bytes=60 * 1024 * 1024),
     )(panel_ids, a_tile, b_tile, c_prior, sketch_matrix)
+    return pl.pallas_call(
+        finish,
+        out_shape=tuple(jax.ShapeDtypeStruct(v.shape, v.dtype) for v in results),
+        in_specs=[hbm] * 3,
+        out_specs=(hbm,) * 3,
+        scratch_shapes=[vmem(v.shape, v.dtype) for v in results] + [dma((2, 3))],
+    )(*results)
 
 
 def solution(mesh):

time: 85.9 us -> 84.6 us (0.985)
  local copies, waits for them, and re-layouts: 3.48 us -> 0 us
  Pallas kernels: 81.6 us -> 83.8 us
    unnamed x7 -> x0, local copies, waits for them, and re-layouts: 3.48 us -> none
    pallas_call x0 -> x1, Pallas kernels: none -> 2.19 us  [per_device(): pl.pallas_call(finish, out_shape=tuple((jax.ShapeDtypeStruct(v.shape, v.d...]
where the time goes in v4:
time: 84.6 us; the launch traced here: 84.4 us
  Pallas kernels  83.8 us (99%)
    pallas_call x1, Pallas kernels, per_device(): pl.pallas_call(functools.partial(kernel, (nz, na, nb, ta, tb, rows_k)), o...  81.6 us
    pallas_call x1, Pallas kernels, per_device(): pl.pallas_call(finish, out_shape=tuple((jax.ShapeDtypeStruct(v.shape, v.d...  2.19 us

profile of v4, /device:TPU:1, one launch (start us, length us, event | category | flops | bytes accessed | tf_op | source)
XLA Modules:
  0.0 84.4 jit_solution(2855353027477871705)
XLA Ops:
  0.6 81.6 %shard_map.76 = (bf16[256,1664]{1,0:T(8,128)(2,1)}, f32[256,128]{1,0:T(8,128)}, f32[256,128]{1,0:T(8,128)}) custom-call(s32[2]{0:T(128)} %ids.1, bf16[256,1024]{1,0:T(8,128)(2,1)} %a_hbm.1, bf16[512,1664]{1,0:T(8,128)(2,1)} %b_hbm.1, bf16[256,1664]{1,0:T(8,128)(2,1)} %c_hbm.1, bf16[1664,128]{1,0:T(8,128)(2,1)} %s_hbm.1), custom_call_target="tpu_custom_call" | custom-call | tf_op jit(solution)/shard_map/pallas_call | solution.py:436
  82.2 2.2 %shard_map.77 = (bf16[256,1664]{1,0:T(8,128)(2,1)}, f32[256,128]{1,0:T(8,128)}, f32[256,128]{1,0:T(8,128)}) custom-call(bf16[256,1664]{1,0:T(8,128)(2,1)} %get-tuple-element.6.refs_0_, f32[256,128]{1,0:T(8,128)} %get-tuple-element.7.refs_1_, f32[256,128]{1,0:T(8,128)} %get-tuple-element.8.refs_2_), custom_call_target="tpu_custom_call" | custom-call | tf_op jit(solution)/shard_map/pallas_call | solution.py:473
